TPU v7x, 128 devices: a whole 4x4x4 slice. The times are simulated.
128 devices in a mesh: req: 8 (over z, core), wide: 16 (over x, y).
Axes of the slice: x: 4, y: 4, z: 4, core: 2. Of those that a mesh axis runs over, the one named last changes fastest.
Arguments:
- queries: bfloat16 [16384, 3072], P(('req', 'wide'))
- suffix_latent: bfloat16 [16384, 512], P(('req', 'wide')), may hold values from -6 to 6
- suffix_rope: bfloat16 [64, 16384], P(None, ('req', 'wide')), may hold values from -6 to 6
- residual: bfloat16 [16384, 2048], P(('req', 'wide')), may hold values from -3 to 3
- prefix_latent: bfloat16 [8, 2, 2048, 512], P('req', None, 'wide'), may hold values from -6 to 6
- prefix_rope: bfloat16 [8, 2, 64, 2048], P('req', None, None, 'wide')
- suffix_lengths: int32 [128, 4], P(('req', 'wide')), may hold values from 1 to 64, 128 in all within a row
- prefix_ids: int32 [128, 4], P(('req', 'wide')), may hold values from 0 to 1
- w_ukv: bfloat16 [512, 4096], replicated, may hold values from -0.25 to 0.25
- w_out: bfloat16 [2048, 2048], replicated, may hold values from -0.5 to 0.5
- norm_gain: bfloat16 [2048], replicated, may hold values from 0.099609375 to 1.8984375
- expert_ids: int32 [16384, 6], P(('req', 'wide')), may hold values from 0 to 63, all different within a row; in each aligned block of 128 rows (0 to 127, 128 to 255, ...) at most 13 rows name the same one
- gate_values: float32 [16384, 6], P(('req', 'wide')), may hold values from 0.05 to 0.45
- expert_gate_up: bfloat16 [128, 2048, 1408], P(('req', 'wide')), may hold values from -0.125 to 0.125
- expert_down: bfloat16 [128, 704, 2048], P(('req', 'wide')), may hold values from -0.15625 to 0.15625
Outputs:
- layer_out: bfloat16 [16384, 2048], P(('req', 'wide'))
Inputs may be any that keep to these rules, and one draw needn't show every extreme that they name: `suffix_lengths`: row b gives, in order, the lengths of the 4 requests that make up tokens b * 128 to (b + 1) * 128 - 1; each row sums to 128 and its largest entry is 64. `expert_ids`: a token's 6 experts differ; among the 128 tokens of one device no expert is named more than 13 times, and in some device one expert is named exactly 13 times.
All inputs are finite; a program needn't handle non-finite values.
Results may differ from a plain program's by a relative error of at most 0.012.
Values may be sent and summed in bfloat16 or wider, within the bound.
No kernel may reach another device: no remote copies, remote signals or barrier semaphores. Data moves between devices by JAX's collectives and lax.ppermute only.
A program may use at most 192 MiB of HBM per device.

v0:
```python
import jax
import jax.numpy as jnp
from jax import lax
from jax.experimental import pallas as pl
from jax.experimental.pallas import tpu as pltpu
from jax.sharding import PartitionSpec as P


D = 2048
HEADS = 16
NOPE = 128
ROPE = 64
LAT = 512
TOP = 6
PREF = 2
EXPERTS = 64
TOK = 128
REQS = 4
TILE = 16
CAP = 13
SLOTS_A = 8
HALF = D // 2
PIECE = D // 8
WIDTH_B = HALF + PIECE
BLK = 144
EPS = 1e-06
SCALE = 1.0 / (NOPE + ROPE) ** 0.5
LOG2E = 1.4426950408889634
NEG = -1e30
bf16 = jnp.bfloat16
f32 = jnp.float32


def request_scalars(sc_ref):
    lens = [sc_ref[r] for r in range(REQS)]
    own = [sc_ref[REQS + r] for r in range(REQS)]
    starts, total = [], 0
    for r in range(REQS):
        starts.append(total)
        total = total + lens[r]
    zero_count = sum(jnp.where(own[r] == 0, lens[r], 0) for r in range(REQS))
    bases, next0, next1 = [], 0, zero_count
    for r in range(REQS):
        is0 = own[r] == 0
        bases.append(jnp.where(is0, next0, next1))
        next0 = next0 + jnp.where(is0, lens[r], 0)
        next1 = next1 + jnp.where(is0, 0, lens[r])
    return lens, starts, bases, zero_count


def place_of(tokens, starts, bases):
    place = tokens - starts[0] + bases[0]
    for r in range(1, REQS):
        place = jnp.where(tokens >= starts[r], tokens - starts[r] + bases[r], place)
    return place


def sort_matrix(sc_ref, transposed):
    _, starts, bases, _ = request_scalars(sc_ref)
    token_dim = 0 if transposed else 1
    tokens = lax.broadcasted_iota(jnp.int32, (TOK, TOK), token_dim)
    slots = lax.broadcasted_iota(jnp.int32, (TOK, TOK), 1 - token_dim)
    return jnp.where(place_of(tokens, starts, bases) == slots, 1.0, 0.0).astype(bf16)


def mm(a, b):
    return jnp.dot(a, b, preferred_element_type=f32)


def mm_nt(a, b):
    return lax.dot_general(a, b, (((1,), (1,)), ((), ())), preferred_element_type=f32)


def mm_tn(a, b):
    return lax.dot_general(a, b, (((0,), (0,)), ((), ())), preferred_element_type=f32)


HG = 4


def query_kernel(sc_ref, q_ref, qr_ref, w_ref, qa_ref, qo_ref):
    order = sort_matrix(sc_ref, False)
    nope = mm(order, q_ref[...]).astype(bf16)
    rope = mm(order, qr_ref[...]).astype(bf16)
    for h in range(HG):
        keys = w_ref[:, h * 256 : h * 256 + 128]
        qa_ref[h] = mm_nt(nope[:, h * 128 : (h + 1) * 128], keys).astype(bf16)
        qo_ref[h] = rope[:, h * ROPE : (h + 1) * ROPE]


def prepare_queries(scalars, queries, w_ukv):
    return pl.pallas_call(
        query_kernel,
        out_shape=(
            jax.ShapeDtypeStruct((HEADS, TOK, LAT), bf16),
            jax.ShapeDtypeStruct((HEADS, TOK, ROPE), bf16),
        ),
        grid_spec=pltpu.PrefetchScalarGridSpec(
            num_scalar_prefetch=1,
            grid=(HEADS // HG,),
            in_specs=[
                pl.BlockSpec((TOK, HG * NOPE), lambda i, s: (0, i)),
                pl.BlockSpec((TOK, HG * ROPE), lambda i, s: (0, HEADS * NOPE // (HG * ROPE) + i)),
                pl.BlockSpec((LAT, HG * 2 * NOPE), lambda i, s: (0, i)),
            ],
            out_specs=[
                pl.BlockSpec((HG, TOK, LAT), lambda i, s: (i, 0, 0)),
                pl.BlockSpec((HG, TOK, ROPE), lambda i, s: (i, 0, 0)),
            ],
        ),
        name="query_prep",
    )(scalars, queries, queries, w_ukv)


ROWS = HEADS * TILE


def block_views(refs):
    views = []
    for ref in refs:
        for b in range(ref.shape[0] // BLK):
            views.append((ref, b * BLK))
    return views


def attention_kernel(n_pieces, sc_ref, qa_ref, qr_ref, ll_ref, lr_ref, *rest):
    pieces = (rest[:n_pieces], rest[n_pieces : 2 * n_pieces])
    o_ref, s_scr, m_scr, l_scr, acc_scr = rest[2 * n_pieces :]
    lens, starts, bases, zero_count = request_scalars(sc_ref)
    first = pl.program_id(0) * TILE
    c = SCALE * LOG2E
    q = qa_ref[...].reshape(ROWS, LAT)
    qr = qr_ref[...].reshape(ROWS, ROPE)

    places = first + lax.broadcasted_iota(jnp.int32, (TILE, TOK), 0)
    keys_at = lax.broadcasted_iota(jnp.int32, (TILE, TOK), 1)
    bias = jnp.full((TILE, TOK), NEG, f32)
    for r in range(REQS):
        mine = (places >= bases[r]) & (places < bases[r] + lens[r])
        tok = places - bases[r] + starts[r]
        ok = mine & (keys_at >= starts[r]) & (keys_at <= tok)
        bias = jnp.where(ok, 0.0, bias)
    local_lat = ll_ref[...]
    s = mm_nt(q, local_lat) + mm(qr, lr_ref[...])
    s = (s.reshape(HEADS, TILE, TOK) + bias[None]).reshape(ROWS, TOK)
    m = jnp.max(s, axis=1, keepdims=True)
    p = jnp.exp2((s - m) * c)
    m_scr[...] = jnp.broadcast_to(m, (ROWS, 128))
    l_scr[...] = jnp.broadcast_to(jnp.sum(p, axis=1, keepdims=True), (ROWS, 128))
    acc_scr[...] = mm(p.astype(bf16), local_lat)

    for pre in range(PREF):
        needed = (first < zero_count) if pre == 0 else (first + TILE > zero_count)

        @pl.when(needed)
        def _(pre=pre):
            views = block_views(pieces[pre])
            place = first + lax.broadcasted_iota(jnp.int32, (ROWS, 1), 0) % TILE
            mine = (place < zero_count) if pre == 0 else (place >= zero_count)
            row_bias = jnp.where(mine, 0.0, NEG)
            per = 4
            chunks = [views[k : k + per] for k in range(0, len(views), per)]
            m_old = m_scr[:, :1]
            m_new = m_old
            for k, chunk in enumerate(chunks):
                lat = jnp.concatenate([ref[at : at + 128, :] for ref, at in chunk], axis=0)
                rope = jnp.concatenate(
                    [
                        jnp.concatenate(
                            [ref[at + 128 : at + 144, j * 128 : (j + 1) * 128] for j in range(4)],
                            axis=0,
                        )
                        for ref, at in chunk
                    ],
                    axis=1,
                )
                s = mm_nt(q, lat) + mm(qr, rope) + row_bias
                s_scr[k] = s
                m_new = jnp.maximum(m_new, jnp.max(s, axis=1, keepdims=True))
            scale_old = jnp.exp2((m_old - m_new) * c)
            total = l_scr[:, :1] * scale_old
            acc = acc_scr[...] * scale_old
            for k, chunk in enumerate(chunks):
                lat = jnp.concatenate([ref[at : at + 128, :] for ref, at in chunk], axis=0)
                p = jnp.exp2((s_scr[k] - m_new) * c)
                total = total + jnp.sum(p, axis=1, keepdims=True)
                acc = acc + mm(p.astype(bf16), lat)
            m_scr[...] = jnp.broadcast_to(m_new, (ROWS, 128))
            l_scr[...] = jnp.broadcast_to(total, (ROWS, 128))
            acc_scr[...] = acc

    out = acc_scr[...] / l_scr[:, :1]
    o_ref[...] = out.astype(bf16).reshape(HEADS, TILE, LAT)


def attend(scalars, qa, qr, local_lat, local_rope, pieces0, pieces1):
    n_pieces = len(pieces0)
    whole = lambda a: pl.BlockSpec(a.shape, lambda i, s: (0,) * a.ndim)
    pieces = [*pieces0, *pieces1]
    return pl.pallas_call(
        lambda *refs: attention_kernel(n_pieces, *refs),
        out_shape=jax.ShapeDtypeStruct((HEADS, TOK, LAT), bf16),
        grid_spec=pltpu.PrefetchScalarGridSpec(
            num_scalar_prefetch=1,
            grid=(TOK // TILE,),
            in_specs=[
                pl.BlockSpec((HEADS, TILE, LAT), lambda i, s: (0, i, 0)),
                pl.BlockSpec((HEADS, TILE, ROPE), lambda i, s: (0, i, 0)),
                whole(local_lat),
                whole(local_rope),
                *[pl.BlockSpec(memory_space=pltpu.VMEM) for _ in pieces],
            ],
            out_specs=pl.BlockSpec((HEADS, TILE, LAT), lambda i, s: (0, i, 0)),
            scratch_shapes=[
                pltpu.VMEM((4, ROWS, 512), f32),
                pltpu.VMEM((ROWS, 128), f32),
                pltpu.VMEM((ROWS, 128), f32),
                pltpu.VMEM((ROWS, LAT), f32),
            ],
        ),
        name="attention",
    )(scalars, qa, qr, local_lat, local_rope, *pieces)


def project_kernel(sc_ref, o_ref, w_ref, wo_ref, res_ref, gain_ref, hid_ref, norm_ref, acc_ref):
    step = pl.program_id(0)

    @pl.when(step == 0)
    def _():
        acc_ref[...] = res_ref[...].astype(f32)

    back = sort_matrix(sc_ref, True)
    heads = [mm(o_ref[h], w_ref[:, h * 256 + 128 : h * 256 + 256]).astype(bf16) for h in range(HG)]
    head_out = mm(back, jnp.concatenate(heads, axis=1)).astype(bf16)
    acc_ref[...] += mm(head_out, wo_ref[...])

    @pl.when(step == HEADS // HG - 1)
    def _():
        hidden = acc_ref[...].astype(bf16)
        hid_ref[...] = hidden
        h32 = hidden.astype(f32)
        inverse = lax.rsqrt(jnp.mean(h32 * h32, axis=1, keepdims=True) + EPS)
        norm_ref[...] = (h32 * inverse * gain_ref[...].astype(f32)).astype(bf16)


def project(scalars, o_lat, w_ukv, w_out, residual, gain):
    return pl.pallas_call(
        project_kernel,
        out_shape=(
            jax.ShapeDtypeStruct((TOK, D), bf16),
            jax.ShapeDtypeStruct((TOK, D), bf16),
        ),
        grid_spec=pltpu.PrefetchScalarGridSpec(
            num_scalar_prefetch=1,
            grid=(HEADS // HG,),
            in_specs=[
                pl.BlockSpec((HG, TOK, LAT), lambda i, s: (i, 0, 0)),
                pl.BlockSpec((LAT, HG * 2 * NOPE), lambda i, s: (0, i)),
                pl.BlockSpec((HG * NOPE, D), lambda i, s: (i, 0)),
                pl.BlockSpec((TOK, D), lambda i, s: (0, 0)),
                pl.BlockSpec((1, D), lambda i, s: (0, 0)),
            ],
            out_specs=[
                pl.BlockSpec((TOK, D), lambda i, s: (0, 0)),
                pl.BlockSpec((TOK, D), lambda i, s: (0, 0)),
            ],
            scratch_shapes=[pltpu.VMEM((TOK, D), f32)],
        ),
        name="project",
    )(scalars, o_lat, w_ukv, w_out, residual, gain)


def rank_table(ids_ref):
    expert = lax.broadcasted_iota(jnp.int32, (EXPERTS, TOK), 0)
    named = ids_ref[0:1, :] == expert
    for k in range(1, TOP):
        named = named | (ids_ref[k : k + 1, :] == expert)
    earlier = lax.broadcasted_iota(jnp.int32, (TOK, TOK), 0) < lax.broadcasted_iota(
        jnp.int32, (TOK, TOK), 1
    )
    rank = mm(jnp.where(named, 1.0, 0.0).astype(bf16), jnp.where(earlier, 1.0, 0.0).astype(bf16))
    return jnp.where(named, rank, -1.0)


def gate_table(ids_ref, gates_ref):
    expert = lax.broadcasted_iota(jnp.int32, (EXPERTS, TOK), 0)
    gates = jnp.zeros((EXPERTS, TOK), f32)
    for k in range(TOP):
        gates = gates + jnp.where(ids_ref[k : k + 1, :] == expert, gates_ref[k : k + 1, :], 0.0)
    return gates


def whole_rows(ranks, experts, copies, values=None):
    slot = lax.broadcasted_iota(jnp.int32, (SLOTS_A, TOK), 0).astype(f32)
    rows = []
    for e in range(experts):
        on = 1.0 if values is None else values[e : e + 1, :]
        rows += [jnp.where(ranks[e : e + 1, :] == slot, on, 0.0)] * copies
    return jnp.concatenate(rows, axis=0)


def packed_rows(ranks, experts, copies, values=None):
    row = lax.broadcasted_iota(jnp.int32, (8, TOK), 0)
    slot = (SLOTS_A + row // 2).astype(f32)
    even = row % 2 == 0
    lower, upper, last = [], [], []
    for e in range(experts):
        rank = ranks[e : e + 1, :]
        on = 1.0 if values is None else values[e : e + 1, :]
        hit = jnp.where(rank == slot, on, 0.0)
        lower += [jnp.where(even, hit, 0.0)] * copies
        upper += [jnp.where(even, 0.0, hit)] * copies
        last += [jnp.where(jnp.broadcast_to(rank, (8, TOK)) == CAP - 1.0, on, 0.0)] * copies
    return [jnp.concatenate(part, axis=0) for part in (lower, upper, last)]


def pieces_of(last):
    row = lax.broadcasted_iota(jnp.int32, last.shape, 0) % 8
    return [jnp.where(row == q, last, 0.0) for q in range(8)]


EG = 16


def dispatch_kernel(ids_ref, norm_ref, out_ref, rank_scr):
    step = pl.program_id(0)

    @pl.when(step == 0)
    def _():
        rank_scr[...] = rank_table(ids_ref)

    ranks = rank_scr[pl.ds(step * EG, EG), :]
    sent = mm(whole_rows(ranks, EG, 1).astype(bf16), norm_ref[...]).astype(bf16)
    for e in range(EG):
        part = sent[e * SLOTS_A : (e + 1) * SLOTS_A]
        out_ref[2 * e] = part
        out_ref[2 * e + 1] = part


def dispatch_packed_kernel(ids_ref, norm_ref, out_ref, rank_scr):
    step = pl.program_id(0)

    @pl.when(step == 0)
    def _():
        rank_scr[...] = rank_table(ids_ref)

    ranks = rank_scr[pl.ds(step * EG, EG), :]
    lower, upper, last = packed_rows(ranks, EG, 1)
    sent = (
        mm(lower.astype(bf16), norm_ref[:, :HALF]) + mm(upper.astype(bf16), norm_ref[:, HALF:])
    ).astype(bf16)
    tail = jnp.zeros((EG * 8, PIECE), f32)
    for q, piece in enumerate(pieces_of(last)):
        tail = tail + mm(piece.astype(bf16), norm_ref[:, q * PIECE : (q + 1) * PIECE])
    tail = tail.astype(bf16)
    for e in range(EG):
        for copy in range(2):
            out_ref[2 * e + copy, :, :HALF] = sent[e * 8 : (e + 1) * 8]
            out_ref[2 * e + copy, :, HALF:] = tail[e * 8 : (e + 1) * 8]


def dispatch(kernel, width, ids_t, normed):
    return pl.pallas_call(
        kernel,
        out_shape=jax.ShapeDtypeStruct((2 * EXPERTS, 8, width), bf16),
        grid=(EXPERTS // EG,),
        in_specs=[
            pl.BlockSpec((TOP, TOK), lambda i: (0, 0)),
            pl.BlockSpec((TOK, D), lambda i: (0, 0)),
        ],
        out_specs=pl.BlockSpec((2 * EG, 8, width), lambda i: (i, 0, 0)),
        scratch_shapes=[pltpu.VMEM((EXPERTS, TOK), f32)],
    )(ids_t, normed)


def activate(x, wg_ref):
    gate_up = mm(x, wg_ref[0])
    gate, up = gate_up[:, :HIDDEN], gate_up[:, HIDDEN:]
    return gate / (1.0 + jnp.exp(-gate)) * up


def up_kernel(side_ref, x_ref, wg_ref, own_ref, other_ref):
    n = x_ref.shape[0] // 2
    act = activate(x_ref[...].reshape(-1, D), wg_ref).reshape(n, 2, 8, HIDDEN)
    even = side_ref[0] == 0
    own_ref[...] = jnp.where(even, act[:, 0], act[:, 1]).astype(bf16)
    other_ref[...] = jnp.where(even, act[:, 1], act[:, 0]).astype(bf16)


def pick(rows, columns, stride, offset):
    r = lax.broadcasted_iota(jnp.int32, (rows, columns), 0)
    c = lax.broadcasted_iota(jnp.int32, (rows, columns), 1)
    return jnp.where(c == r * stride + offset, 1.0, 0.0).astype(bf16)


def pick_main(n, side, half):
    r = lax.broadcasted_iota(jnp.int32, (4 * n, 16 * n), 0)
    c = lax.broadcasted_iota(jnp.int32, (4 * n, 16 * n), 1)
    at = (2 * (r // 4) + side) * 8 + 2 * (r % 4) + half
    return jnp.where(c == at, 1.0, 0.0).astype(bf16)


def up_packed_kernel(side_ref, x_ref, wg_ref, own_ref, other_ref):
    n = x_ref.shape[0] // 2
    x = x_ref[...].reshape(16 * n, WIDTH_B)
    wide, tail = x[:, :HALF], x[:, HALF:]
    own, other = side_ref[0], 1 - side_ref[0]
    halves = [
        mm(jnp.concatenate([pick_main(n, own, h), pick_main(n, other, h)], axis=0), wide)
        for h in range(2)
    ]
    main = jnp.concatenate(halves, axis=1)
    parts = []
    for q in range(8):
        chosen = [pick(n, 16 * n, 16, 8 * own + q), pick(n, 16 * n, 16, 8 * other + q)]
        parts.append(mm(jnp.concatenate(chosen, axis=0), tail))
    last = jnp.concatenate(parts, axis=1)
    act = activate(jnp.concatenate([main, last], axis=0).astype(bf16), wg_ref).astype(bf16)
    own_ref[0, : 4 * n] = act[: 4 * n]
    own_ref[0, 4 * n :] = act[8 * n : 9 * n]
    other_ref[0, : 4 * n] = act[4 * n : 8 * n]
    other_ref[0, 4 * n :] = act[9 * n :]


PER = 16
HIDDEN = 704


def run_up(kernel, side, rows, w_gate_up):
    width = rows.shape[2]
    steps = rows.shape[0] // (2 * PER)
    if width == D:
        shape, block = (PER * steps, 8, HIDDEN), (PER, 8, HIDDEN)
    else:
        shape, block = (steps, 5 * PER, HIDDEN), (1, 5 * PER, HIDDEN)
    return pl.pallas_call(
        kernel,
        out_shape=(jax.ShapeDtypeStruct(shape, bf16),) * 2,
        grid_spec=pltpu.PrefetchScalarGridSpec(
            num_scalar_prefetch=1,
            grid=(steps,),
            in_specs=[
                pl.BlockSpec((2 * PER, 8, width), lambda i, s: (i, 0, 0)),
                pl.BlockSpec(
                    w_gate_up.shape, lambda i, s: (0, 0, 0), pipeline_mode=pl.Buffered(1)
                ),
            ],
            out_specs=[pl.BlockSpec(block, lambda i, s: (i, 0, 0))] * 2,
        ),
    )(side, rows, w_gate_up)


def down_kernel(own_ref, came_ref, wo_ref, wc_ref, out_ref):
    own = own_ref[...].reshape(-1, HIDDEN)
    came = came_ref[...].reshape(-1, HIDDEN)
    out = mm(own, wo_ref[0]) + mm(came, wc_ref[0])
    out_ref[...] = out.astype(bf16).reshape(out_ref.shape)


def down_packed_kernel(own_ref, came_ref, wo_ref, wc_ref, out_ref):
    n = out_ref.shape[0]
    y = (mm(own_ref[0], wo_ref[0]) + mm(came_ref[0], wc_ref[0])).astype(bf16)
    main, last = y[: 4 * n], y[4 * n :]
    even, odd = pick(4 * n, 8 * n, 2, 0), pick(4 * n, 8 * n, 2, 1)
    out = mm_tn(even, main[:, :HALF]) + mm_tn(odd, main[:, HALF:])
    tail = jnp.zeros((8 * n, PIECE), f32)
    for q in range(8):
        tail = tail + mm_tn(pick(n, 8 * n, 8, q), last[:, q * PIECE : (q + 1) * PIECE])
    out_ref[:, :, :HALF] = out.astype(bf16).reshape(n, 8, HALF)
    out_ref[:, :, HALF:] = tail.astype(bf16).reshape(n, 8, PIECE)


def run_down(kernel, own, came, w_own, w_came, width):
    blocks = 2 if width == D else 1
    steps = EXPERTS // PER // blocks
    act = pl.BlockSpec((own.shape[0] // steps, *own.shape[1:]), lambda i: (i, 0, 0))
    weight = pl.BlockSpec(w_own.shape, lambda i: (0, 0, 0), pipeline_mode=pl.Buffered(1))
    return pl.pallas_call(
        kernel,
        out_shape=jax.ShapeDtypeStruct((EXPERTS, 8, width), bf16),
        grid=(steps,),
        in_specs=[act, act, weight, weight],
        out_specs=pl.BlockSpec((EXPERTS // steps, 8, width), lambda i: (i, 0, 0)),
    )(own, came, w_own, w_came)


def weighted(weight, back):
    high = weight.astype(bf16)
    low = (weight - high.astype(f32)).astype(bf16)
    both = mm_tn(jnp.concatenate([high, low], axis=1), back)
    return both[:TOK] + both[TOK:]


CG = 32


def combine_kernel(ids_ref, gates_ref, hid_ref, back_ref, out_ref, rank_scr, gate_scr):
    step = pl.program_id(0)

    @pl.when(step == 0)
    def _():
        rank_scr[...] = rank_table(ids_ref)
        gate_scr[...] = gate_table(ids_ref, gates_ref)
        out_ref[...] = hid_ref[...].astype(f32)

    ranks = rank_scr[pl.ds(step * CG, CG), :]
    gates = gate_scr[pl.ds(step * CG, CG), :]
    back = back_ref[...].reshape(CG * SLOTS_A, D)
    out_ref[...] += weighted(whole_rows(ranks, CG, 1, gates), back)


def combine(ids_t, gates_t, hidden, back):
    return pl.pallas_call(
        combine_kernel,
        out_shape=jax.ShapeDtypeStruct((TOK, D), f32),
        grid=(EXPERTS // CG,),
        in_specs=[
            pl.BlockSpec((TOP, TOK), lambda i: (0, 0)),
            pl.BlockSpec((TOP, TOK), lambda i: (0, 0)),
            pl.BlockSpec((TOK, D), lambda i: (0, 0)),
            pl.BlockSpec((CG, 8, D), lambda i: (i, 0, 0)),
        ],
        out_specs=pl.BlockSpec((TOK, D), lambda i: (0, 0)),
        scratch_shapes=[pltpu.VMEM((EXPERTS, TOK), f32), pltpu.VMEM((EXPERTS, TOK), f32)],
        name="combine_a",
    )(ids_t, gates_t, hidden, back)


def combine_packed_kernel(ids_ref, gates_ref, sum_ref, back_ref, out_ref, acc_ref):
    ranks = rank_table(ids_ref)
    gates = gate_table(ids_ref, gates_ref)
    back = back_ref[...].reshape(EXPERTS * 8, WIDTH_B)
    lower, upper, last = packed_rows(ranks, EXPERTS, 1, gates)
    acc_ref[:, :HALF] = sum_ref[:, :HALF] + weighted(lower, back[:, :HALF])
    acc_ref[:, HALF:] = sum_ref[:, HALF:] + weighted(upper, back[:, :HALF])
    for q, piece in enumerate(pieces_of(last)):
        acc_ref[:, q * PIECE : (q + 1) * PIECE] += weighted(piece, back[:, HALF:])
    out_ref[...] = acc_ref[...].astype(bf16)


def combine_packed(ids_t, gates_t, base, back):
    return pl.pallas_call(
        combine_packed_kernel,
        out_shape=jax.ShapeDtypeStruct((TOK, D), bf16),
        in_specs=[pl.BlockSpec(memory_space=pltpu.VMEM)] * 4,
        out_specs=pl.BlockSpec(memory_space=pltpu.VMEM),
        scratch_shapes=[pltpu.VMEM((TOK, D), f32)],
        name="combine_b",
    )(ids_t, gates_t, base, back)


def shift(axis, k):
    pairs = []
    for x in range(4):
        for y in range(4):
            tx, ty = ((x + k) % 4, y) if axis == "x" else (x, (y + k) % 4)
            pairs.append((x * 4 + y, tx * 4 + ty))
    return pairs


def hop(a, axis, k):
    return lax.ppermute(a, "wide", shift(axis, k))


def gather_row(own, first):
    ahead, behind = hop(own, first, 1), hop(own, first, -1)
    far = hop(own, first, 2)
    return jnp.concatenate([own, ahead, behind, far], axis=0)


def gather_rest(row, second):
    ahead, behind = hop(row, second, 1), hop(row, second, -1)
    far = hop(row, second, 2)
    return [row, ahead, behind, far]


def swap(a):
    return lax.ppermute(a, "wide", [(w, w ^ 1) for w in range(16)])


def pack_prefix(latent, rope):
    packed = rope.reshape(4, 16, TOK).transpose(1, 0, 2).reshape(16, 4 * TOK)
    return jnp.concatenate([latent, packed], axis=0)


def exchange(a):
    return lax.all_to_all(a, ("req", "wide"), split_axis=0, concat_axis=0, tiled=True)


def give_back(a):
    sides = [list(range(side, 2 * EXPERTS, 2)) for side in range(2)]
    return lax.all_to_all(
        a, ("req", "wide"), split_axis=0, concat_axis=0, axis_index_groups=sides, tiled=True
    )


def layer(
    queries,
    suffix_latent,
    suffix_rope,
    residual,
    prefix_latent,
    prefix_rope,
    suffix_lengths,
    prefix_ids,
    w_ukv,
    w_out,
    norm_gain,
    expert_ids,
    gate_values,
    expert_gate_up,
    expert_down,
):
    scalars = jnp.concatenate([suffix_lengths[0], prefix_ids[0]])
    row0 = gather_row(pack_prefix(prefix_latent[0, 0], prefix_rope[0, 0]), "x")
    row1 = gather_row(pack_prefix(prefix_latent[0, 1], prefix_rope[0, 1]), "y")
    pieces0 = gather_rest(row0, "y")
    pieces1 = gather_rest(row1, "x")
    down_came = swap(expert_down)
    side = (lax.axis_index("wide") % 2).reshape(1)
    qa, qr = prepare_queries(scalars, queries, w_ukv)
    o_lat = attend(scalars, qa, qr, suffix_latent, suffix_rope, pieces0, pieces1)
    hidden, normed = project(scalars, o_lat, w_ukv, w_out, residual, norm_gain.reshape(1, D))
    ids_t = expert_ids.T
    gates_t = gate_values.T
    sent_a = dispatch(dispatch_kernel, D, ids_t, normed)
    sent_b = dispatch(dispatch_packed_kernel, WIDTH_B, ids_t, normed)
    rows_a = exchange(sent_a)
    rows_b = exchange(sent_b)
    own_a, other_a = run_up(up_kernel, side, rows_a, expert_gate_up)
    came_a = swap(other_a)
    made_a = run_down(down_kernel, own_a, came_a, expert_down, down_came, D)
    own_b, other_b = run_up(up_packed_kernel, side, rows_b, expert_gate_up)
    came_b = swap(other_b)
    made_b = run_down(down_packed_kernel, own_b, came_b, expert_down, down_came, WIDTH_B)
    back_a = give_back(made_a)
    back_b = give_back(made_b)
    part = combine(ids_t, gates_t, hidden, back_a)
    return combine_packed(ids_t, gates_t, part, back_b)


def solution(mesh):
    return jax.shard_map(
        layer,
        mesh=mesh,
        in_specs=(
            P(("req", "wide"), None),
            P(("req", "wide"), None),
            P(None, ("req", "wide")),
            P(("req", "wide"), None),
            P("req", None, "wide", None),
            P("req", None, None, "wide"),
            P(("req", "wide"), None),
            P(("req", "wide"), None),
            P(),
            P(),
            P(),
            P(("req", "wide"), None),
            P(("req", "wide"), None),
            P(("req", "wide"), None, None),
            P(("req", "wide"), None, None),
        ),
        out_specs=P(("req", "wide"), None),
        check_vma=False,
    )
```

profile of v0, /device:TPU:37, one launch (start us, length us, event | category | flops | bytes accessed | tf_op | source)
XLA Modules:
  0.0 361.5 jit_solution(7827258702883254473)
XLA Ops:
  16.0 10.9 %collective-permute-done.6 = bf16[144,512]{1,0:T(8,128)(2,1)S(1)} collective-permute-done((bf16[144,512]{1,0:T(8,128)(2,1)S(1)}, bf16[144,512]{1,0:T(8,128)(2,1)S(1)}, u32[]{:S(2)}, u32[]{:S(2)}) %collective-permute-start.6) | collective-permute-done | bytes 147488 | tf_op jit(solution)/shard_map/ppermute | solution.py:562
  30.9 2.3 collective-permute-start.9
  33.4 3.5 collective-permute-start.11
  38.2 5.9 %query_prep.1 = (bf16[16,128,512]{2,1,0:T(8,128)(2,1)}, bf16[16,128,64]{2,1,0:T(8,128)(2,1)}) custom-call(s32[8]{0:T(128)} %pad_add_fusion.sc_ref.refs_0_, bf16[128,3072]{1,0:T(8,128)(2,1)} %qr_ref.1, bf16[128,3072]{1,0:T(8,128)(2,1)} %qr_ref.1, bf16[512,4096]{1,0:T(8,128)(2,1)} %w_ref.3), custom_call_target="tpu_custom_call" | custom-call | tf_op jit(solution)/shard_map/query_prep/pallas_call | solution.py:92
  44.2 6.2 %collective-permute-done.11.refs_12_ = bf16[576,512]{1,0:T(8,128)(2,1)} collective-permute-done((bf16[576,512]{1,0:T(8,128)(2,1)S(1)}, bf16[576,512]{1,0:T(8,128)(2,1)}, u32[]{:S(2)}, u32[]{:S(2)}) %collective-permute-start.11) | collective-permute-done | bytes 589856 | tf_op jit(solution)/shard_map/ppermute | solution.py:562
  50.3 26.1 %attention.1.o_ref = bf16[16,128,512]{2,1,0:T(8,128)(2,1)} custom-call(s32[8]{0:T(128)} %pad_add_fusion.sc_ref.refs_0_, bf16[16,128,512]{2,1,0:T(8,128)(2,1)} %get-tuple-element.13.refs_1_, bf16[16,128,64]{2,1,0:T(8,128)(2,1)} %get-tuple-element.14.refs_2_, bf16[128,512]{1,0:T(8,128)(2,1)} %refs_3_.1, bf16[64,128]{1,0:T(8,128)(2,1)} %refs_4_.1, ...), custom_call_target="tpu_custom_call" | custom-call | tf_op jit(solution)/shard_map/attention/pallas_call | solution.py:200
  76.4 9.5 %project.1 = (bf16[128,2048]{1,0:T(8,128)(2,1)}, bf16[128,2048]{1,0:T(8,128)(2,1)}) custom-call(s32[8]{0:T(128)} %pad_add_fusion.sc_ref.refs_0_, bf16[16,128,512]{2,1,0:T(8,128)(2,1)} %attention.1.o_ref, bf16[512,4096]{1,0:T(8,128)(2,1)} %w_ref.3, bf16[2048,2048]{1,0:T(8,128)(2,1)} %wo_ref.3, bf16[128,2048]{1,0:T(8,128)(2,1)} %res_ref.1, ...), custom_call_target="tpu_custom_call" | custom-call | tf_op jit(solution)/shard_map/project/pallas_call | solution.py:247
  85.9 4.2 %shard_map.145 = bf16[128,8,2048]{2,1,0:T(8,128)(2,1)} custom-call(s32[6,128]{1,0:T(8,128)} %bitcast.37, bf16[128,2048]{1,0:T(8,128)(2,1)} %get-tuple-element.16.norm_ref), custom_call_target="tpu_custom_call" | custom-call | tf_op jit(solution)/shard_map/pallas_call | solution.py:363
  90.2 20.9 %all-to-all-start = ((bf16[128,8,2048]{2,1,0:T(8,128)(2,1)}), bf16[128,8,2048]{2,1,0:T(8,128)(2,1)}, u32[]{:S(2)}, u32[]{:S(2)}) async-start(bf16[128,8,2048]{2,1,0:T(8,128)(2,1)} %shard_map.145), calls=%async_computation | async-start | bytes 8388608 | tf_op jit(solution)/shard_map/all_to_all | solution.py:587
  112.5 4.2 %shard_map.148 = bf16[128,8,1280]{2,1,0:T(8,128)(2,1)} custom-call(s32[6,128]{1,0:T(8,128)} %bitcast.38, bf16[128,2048]{1,0:T(8,128)(2,1)} %get-tuple-element.16.norm_ref), custom_call_target="tpu_custom_call" | custom-call | tf_op jit(solution)/shard_map/pallas_call | solution.py:363
  116.7 44.5 %all-to-all-done.x_ref = bf16[128,8,2048]{2,1,0:T(8,128)(2,1)} async-done(((bf16[128,8,2048]{2,1,0:T(8,128)(2,1)}), bf16[128,8,2048]{2,1,0:T(8,128)(2,1)}, u32[]{:S(2)}, u32[]{:S(2)}) %all-to-all-start) | async-done | bytes 4194336 | tf_op jit(solution)/shard_map/all_to_all | solution.py:587
  161.2 6.8 %all-to-all-start.2 = ((bf16[128,8,1280]{2,1,0:T(8,128)(2,1)}), bf16[128,8,1280]{2,1,0:T(8,128)(2,1)}, u32[]{:S(2)}, u32[]{:S(2)}) async-start(bf16[128,8,1280]{2,1,0:T(8,128)(2,1)} %shard_map.148), calls=%async_computation.2 | async-start | bytes 5242880 | tf_op jit(solution)/shard_map/all_to_all | solution.py:587
  168.1 11.5 %shard_map.146 = (bf16[64,8,704]{2,1,0:T(8,128)(2,1)}, bf16[64,8,704]{2,1,0:T(8,128)(2,1)}) custom-call(s32[1]{0:T(128)} %bitcast.10.side_ref, bf16[128,8,2048]{2,1,0:T(8,128)(2,1)} %all-to-all-done.x_ref, bf16[1,2048,1408]{2,1,0:T(8,128)(2,1)} %wg_ref.3), custom_call_target="tpu_custom_call" | custom-call | tf_op jit(solution)/shard_map/pallas_call | solution.py:436
  180.9 59.5 %collective-permute-done.13.wc_ref = bf16[1,704,2048]{2,1,0:T(8,128)(2,1)} collective-permute-done((bf16[1,704,2048]{2,1,0:T(8,128)(2,1)S(1)}, bf16[1,704,2048]{2,1,0:T(8,128)(2,1)}, u32[]{:S(2)}, u32[]{:S(2)}) %collective-permute-start.13) | collective-permute-done | bytes 2883616 | tf_op jit(solution)/shard_map/ppermute | solution.py:578
  240.3 23.9 %collective-permute-done.12.came_ref = bf16[64,8,704]{2,1,0:T(8,128)(2,1)} collective-permute-done((bf16[64,8,704]{2,1,0:T(8,128)(2,1)}, bf16[64,8,704]{2,1,0:T(8,128)(2,1)}, u32[]{:S(2)}, u32[]{:S(2)}) %collective-permute-start.12) | collective-permute-done | bytes 720928 | tf_op jit(solution)/shard_map/ppermute | solution.py:578
  264.2 7.5 %shard_map.147 = bf16[64,8,2048]{2,1,0:T(8,128)(2,1)} custom-call(bf16[64,8,704]{2,1,0:T(8,128)(2,1)} %get-tuple-element.17.own_ref, bf16[64,8,704]{2,1,0:T(8,128)(2,1)} %collective-permute-done.12.came_ref, bf16[1,704,2048]{2,1,0:T(8,128)(2,1)} %wo_ref.5, bf16[1,704,2048]{2,1,0:T(8,128)(2,1)} %collective-permute-done.13.wc_ref), custom_call_target="tpu_custom_call" | custom-call | tf_op jit(solution)/shard_map/pallas_call | solution.py:478
  271.7 10.4 %all-to-all-start.1 = ((bf16[64,8,2048]{2,1,0:T(8,128)(2,1)}), bf16[64,8,2048]{2,1,0:T(8,128)(2,1)S(1)}, u32[]{:S(2)}, u32[]{:S(2)}) async-start(bf16[64,8,2048]{2,1,0:T(8,128)(2,1)} %shard_map.147), calls=%async_computation.1 | async-start | bytes 4194304 | tf_op jit(solution)/shard_map/all_to_all | solution.py:592
  282.1 10.2 %shard_map.149 = (bf16[4,80,704]{2,1,0:T(8,128)(2,1)}, bf16[4,80,704]{2,1,0:T(8,128)(2,1)}) custom-call(s32[1]{0:T(128)} %bitcast.10.side_ref, bf16[128,8,1280]{2,1,0:T(8,128)(2,1)} %all-to-all-done.2.x_ref, bf16[1,2048,1408]{2,1,0:T(8,128)(2,1)} %wg_ref.3), custom_call_target="tpu_custom_call" | custom-call | tf_op jit(solution)/shard_map/pallas_call | solution.py:436
  292.3 23.6 %collective-permute-done.14.came_ref = bf16[4,80,704]{2,1,0:T(8,128)(2,1)S(1)} collective-permute-done((bf16[4,80,704]{2,1,0:T(8,128)(2,1)}, bf16[4,80,704]{2,1,0:T(8,128)(2,1)S(1)}, u32[]{:S(2)}, u32[]{:S(2)}) %collective-permute-start.14) | collective-permute-done | bytes 450592 | tf_op jit(solution)/shard_map/ppermute | solution.py:578
  316.7 9.0 %shard_map.150 = bf16[64,8,1280]{2,1,0:T(8,128)(2,1)} custom-call(bf16[4,80,704]{2,1,0:T(8,128)(2,1)} %get-tuple-element.19.own_ref, bf16[4,80,704]{2,1,0:T(8,128)(2,1)} %copy-done.9, bf16[1,704,2048]{2,1,0:T(8,128)(2,1)} %wo_ref.5, bf16[1,704,2048]{2,1,0:T(8,128)(2,1)} %collective-permute-done.13.wc_ref), custom_call_target="tpu_custom_call" | custom-call | tf_op jit(solution)/shard_map/pallas_call | solution.py:478
  325.7 12.2 %all-to-all-start.3 = ((bf16[64,8,1280]{2,1,0:T(8,128)(2,1)}), bf16[64,8,1280]{2,1,0:T(8,128)(2,1)S(1)}, u32[]{:S(2)}, u32[]{:S(2)}) async-start(bf16[64,8,1280]{2,1,0:T(8,128)(2,1)} %shard_map.150), calls=%async_computation.3 | async-start | bytes 2621440 | tf_op jit(solution)/shard_map/all_to_all | solution.py:592
  338.0 3.5 combine_a.1.sum_ref
  341.5 15.0 %all-to-all-done.3.back_ref = bf16[64,8,1280]{2,1,0:T(8,128)(2,1)S(1)} async-done(((bf16[64,8,1280]{2,1,0:T(8,128)(2,1)}), bf16[64,8,1280]{2,1,0:T(8,128)(2,1)S(1)}, u32[]{:S(2)}, u32[]{:S(2)}) %all-to-all-start.3) | async-done | bytes 1310752 | tf_op jit(solution)/shard_map/all_to_all | solution.py:592
  357.6 3.9 %combine_b.1 = bf16[128,2048]{1,0:T(8,128)(2,1)} custom-call(s32[6,128]{1,0:T(8,128)} %bitcast.40, f32[6,128]{1,0:T(8,128)} %bitcast.42, f32[128,2048]{1,0:T(8,128)} %combine_a.1.sum_ref, bf16[64,8,1280]{2,1,0:T(8,128)(2,1)} %copy-done.2), custom_call_target="tpu_custom_call" | custom-call | tf_op jit(solution)/shard_map/combine_b/pallas_call | solution.py:542
  (70 shorter events, 25.9 us)
Async XLA Ops:
  0.0 36.9 %copy-start.10 = (bf16[2048]{0:T(1024)(128)(2,1)S(1)}, bf16[2048]{0:T(1024)(128)(2,1)}, u32[]{:S(2)}) copy-start(bf16[2048]{0:T(1024)(128)(2,1)} %param.25) | copy-start | bytes 12292
  0.0 37.5 %copy-start.11 = (s32[1,4]{1,0:T(1,128)S(1)}, s32[1,4]{1,0:T(1,128)}, u32[]{:S(2)}) copy-start(s32[1,4]{1,0:T(1,128)} %param.22) | copy-start | bytes 52
  0.0 37.5 %copy-start.12 = (s32[1,4]{1,0:T(1,128)S(1)}, s32[1,4]{1,0:T(1,128)}, u32[]{:S(2)}) copy-start(s32[1,4]{1,0:T(1,128)} %param.21) | copy-start | bytes 52
  1.8 4.8 %collective-permute-start = (bf16[144,512]{1,0:T(8,128)(2,1)S(1)}, bf16[144,512]{1,0:T(8,128)(2,1)S(1)}, u32[]{:S(2)}, u32[]{:S(2)}) collective-permute-start(bf16[144,512]{1,0:T(8,128)(2,1)S(1)} %pad_maximum_fusion), channel_id=1, source_target_pairs={{0,4},{1,5},{2,6},{3,7},{4,8},{5,9},{6,10},{7,11},{8,12},{9,13},{1... | collective-permute-start | bytes 442376 | tf_op jit(solution)/shard_map/ppermute | solution.py:562
  2.8 4.5 %collective-permute-start.1 = (bf16[144,512]{1,0:T(8,128)(2,1)S(1)}, bf16[144,512]{1,0:T(8,128)(2,1)S(1)}, u32[]{:S(2)}, u32[]{:S(2)}) collective-permute-start(bf16[144,512]{1,0:T(8,128)(2,1)S(1)} %pad_maximum_fusion), channel_id=1, source_target_pairs={{0,12},{1,13},{2,14},{3,15},{4,0},{5,1},{6,2},{7,3},{8,4},{9,5},{1... | collective-permute-start | bytes 442376 | tf_op jit(solution)/shard_map/ppermute | solution.py:562
  3.4 6.0 %collective-permute-start.2 = (bf16[144,512]{1,0:T(8,128)(2,1)S(1)}, bf16[144,512]{1,0:T(8,128)(2,1)S(1)}, u32[]{:S(2)}, u32[]{:S(2)}) collective-permute-start(bf16[144,512]{1,0:T(8,128)(2,1)S(1)} %pad_maximum_fusion), channel_id=1, source_target_pairs={{0,8},{1,9},{2,10},{3,11},{4,12},{5,13},{6,14},{7,15},{8,0},{9,1},... | collective-permute-start | bytes 442376 | tf_op jit(solution)/shard_map/ppermute | solution.py:562
  9.4 34.7 %copy-start.4 = (bf16[576,512]{1,0:T(8,128)(2,1)}, bf16[576,512]{1,0:T(8,128)(2,1)S(1)}, u32[]{:S(2)}) copy-start(bf16[576,512]{1,0:T(8,128)(2,1)S(1)} %constant_dynamic-update-slice_fusion.refs_5_) | copy-start | bytes 1769476
  9.4 24.1 %collective-permute-start.3 = (bf16[576,512]{1,0:T(8,128)(2,1)S(1)}, bf16[576,512]{1,0:T(8,128)(2,1)S(1)}, u32[]{:S(2)}, u32[]{:S(2)}) collective-permute-start(bf16[576,512]{1,0:T(8,128)(2,1)S(1)} %constant_dynamic-update-slice_fusion.refs_5_), channel_id=1, source_target_pairs={{0,1},{1,2},{2,3},{3,0},{4,5},{5,6},{6,7},{7,4},{8,9},{9,10},{10,1... | collective-permute-start | bytes 1769480 | tf_op jit(solution)/shard_map/ppermute | solution.py:562
  10.8 16.1 %collective-permute-start.6 = (bf16[144,512]{1,0:T(8,128)(2,1)S(1)}, bf16[144,512]{1,0:T(8,128)(2,1)S(1)}, u32[]{:S(2)}, u32[]{:S(2)}) collective-permute-start(bf16[144,512]{1,0:T(8,128)(2,1)S(1)} %pad_maximum_fusion.1), channel_id=1, source_target_pairs={{0,1},{1,2},{2,3},{3,0},{4,5},{5,6},{6,7},{7,4},{8,9},{9,10},{10,1... | collective-permute-start | bytes 442376 | tf_op jit(solution)/shard_map/ppermute | solution.py:562
  12.1 16.4 %collective-permute-start.7 = (bf16[144,512]{1,0:T(8,128)(2,1)S(1)}, bf16[144,512]{1,0:T(8,128)(2,1)S(1)}, u32[]{:S(2)}, u32[]{:S(2)}) collective-permute-start(bf16[144,512]{1,0:T(8,128)(2,1)S(1)} %pad_maximum_fusion.1), channel_id=1, source_target_pairs={{0,3},{1,0},{2,1},{3,2},{4,7},{5,4},{6,5},{7,6},{8,11},{9,8},{10,9... | collective-permute-start | bytes 442376 | tf_op jit(solution)/shard_map/ppermute | solution.py:562
  13.5 17.3 %collective-permute-start.8 = (bf16[144,512]{1,0:T(8,128)(2,1)S(1)}, bf16[144,512]{1,0:T(8,128)(2,1)S(1)}, u32[]{:S(2)}, u32[]{:S(2)}) collective-permute-start(bf16[144,512]{1,0:T(8,128)(2,1)S(1)} %pad_maximum_fusion.1), channel_id=1, source_target_pairs={{0,2},{1,3},{2,0},{3,1},{4,6},{5,7},{6,4},{7,5},{8,10},{9,11},{10,... | collective-permute-start | bytes 442376 | tf_op jit(solution)/shard_map/ppermute | solution.py:562
  14.9 29.2 %collective-permute-start.4 = (bf16[576,512]{1,0:T(8,128)(2,1)S(1)}, bf16[576,512]{1,0:T(8,128)(2,1)S(1)}, u32[]{:S(2)}, u32[]{:S(2)}) collective-permute-start(bf16[576,512]{1,0:T(8,128)(2,1)S(1)} %constant_dynamic-update-slice_fusion.refs_5_), channel_id=1, source_target_pairs={{0,3},{1,0},{2,1},{3,2},{4,7},{5,4},{6,5},{7,6},{8,11},{9,8},{10,9... | collective-permute-start | bytes 1769480 | tf_op jit(solution)/shard_map/ppermute | solution.py:562
  26.9 17.2 %collective-permute-start.5 = (bf16[576,512]{1,0:T(8,128)(2,1)S(1)}, bf16[576,512]{1,0:T(8,128)(2,1)S(1)}, u32[]{:S(2)}, u32[]{:S(2)}) collective-permute-start(bf16[576,512]{1,0:T(8,128)(2,1)S(1)} %constant_dynamic-update-slice_fusion.refs_5_), channel_id=1, source_target_pairs={{0,2},{1,3},{2,0},{3,1},{4,6},{5,7},{6,4},{7,5},{8,10},{9,11},{10,... | collective-permute-start | bytes 1769480 | tf_op jit(solution)/shard_map/ppermute | solution.py:562
  30.9 13.2 %collective-permute-start.9 = (bf16[576,512]{1,0:T(8,128)(2,1)S(1)}, bf16[576,512]{1,0:T(8,128)(2,1)S(1)}, u32[]{:S(2)}, u32[]{:S(2)}) collective-permute-start(bf16[576,512]{1,0:T(8,128)(2,1)S(1)} %constant_dynamic-update-slice_fusion.5.refs_9_), channel_id=1, source_target_pairs={{0,4},{1,5},{2,6},{3,7},{4,8},{5,9},{6,10},{7,11},{8,12},{9,13},{1... | collective-permute-start | bytes 1769480 | tf_op jit(solution)/shard_map/ppermute | solution.py:562
  33.2 11.0 %collective-permute-start.10 = (bf16[576,512]{1,0:T(8,128)(2,1)S(1)}, bf16[576,512]{1,0:T(8,128)(2,1)}, u32[]{:S(2)}, u32[]{:S(2)}) collective-permute-start(bf16[576,512]{1,0:T(8,128)(2,1)S(1)} %constant_dynamic-update-slice_fusion.5.refs_9_), channel_id=1, source_target_pairs={{0,12},{1,13},{2,14},{3,15},{4,0},{5,1},{6,2},{7,3},{8,4},{9,5},{1... | collective-permute-start | bytes 1769480 | tf_op jit(solution)/shard_map/ppermute | solution.py:562
  33.4 16.9 %collective-permute-start.11 = (bf16[576,512]{1,0:T(8,128)(2,1)S(1)}, bf16[576,512]{1,0:T(8,128)(2,1)}, u32[]{:S(2)}, u32[]{:S(2)}) collective-permute-start(bf16[576,512]{1,0:T(8,128)(2,1)S(1)} %constant_dynamic-update-slice_fusion.5.refs_9_), channel_id=1, source_target_pairs={{0,8},{1,9},{2,10},{3,11},{4,12},{5,13},{6,14},{7,15},{8,0},{9,1},... | collective-permute-start | bytes 1769480 | tf_op jit(solution)/shard_map/ppermute | solution.py:562
  90.2 21.0 %copy-start = (bf16[1,704,2048]{2,1,0:T(8,128)(2,1)S(1)}, bf16[1,704,2048]{2,1,0:T(8,128)(2,1)}, u32[]{:S(2)}) copy-start(bf16[1,704,2048]{2,1,0:T(8,128)(2,1)} %wo_ref.5) | copy-start | bytes 8650756
  90.2 71.0 %all-to-all-start = ((bf16[128,8,2048]{2,1,0:T(8,128)(2,1)}), bf16[128,8,2048]{2,1,0:T(8,128)(2,1)}, u32[]{:S(2)}, u32[]{:S(2)}) async-start(bf16[128,8,2048]{2,1,0:T(8,128)(2,1)} %shard_map.145), calls=%async_computation | async-start | bytes 8388608 | tf_op jit(solution)/shard_map/all_to_all | solution.py:587
  111.1 129.2 %collective-permute-start.13 = (bf16[1,704,2048]{2,1,0:T(8,128)(2,1)S(1)}, bf16[1,704,2048]{2,1,0:T(8,128)(2,1)}, u32[]{:S(2)}, u32[]{:S(2)}) collective-permute-start(bf16[1,704,2048]{2,1,0:T(8,128)(2,1)S(1)} %copy-done), channel_id=1, source_target_pairs={{0,1},{1,0},{2,3},{3,2},{4,5},{5,4},{6,7},{7,6},{8,9},{9,8},{10,11... | collective-permute-start | bytes 8650760 | tf_op jit(solution)/shard_map/ppermute | solution.py:578
  161.2 110.5 %all-to-all-start.2 = ((bf16[128,8,1280]{2,1,0:T(8,128)(2,1)}), bf16[128,8,1280]{2,1,0:T(8,128)(2,1)}, u32[]{:S(2)}, u32[]{:S(2)}) async-start(bf16[128,8,1280]{2,1,0:T(8,128)(2,1)} %shard_map.148), calls=%async_computation.2 | async-start | bytes 5242880 | tf_op jit(solution)/shard_map/all_to_all | solution.py:587
  179.6 84.6 %collective-permute-start.12 = (bf16[64,8,704]{2,1,0:T(8,128)(2,1)}, bf16[64,8,704]{2,1,0:T(8,128)(2,1)}, u32[]{:S(2)}, u32[]{:S(2)}) collective-permute-start(bf16[64,8,704]{2,1,0:T(8,128)(2,1)} %get-tuple-element.18), channel_id=1, source_target_pairs={{0,1},{1,0},{2,3},{3,2},{4,5},{5,4},{6,7},{7,6},{8,9},{9,8},{10,11... | collective-permute-start | bytes 2162696 | tf_op jit(solution)/shard_map/ppermute | solution.py:578
  271.7 54.0 %all-to-all-start.1 = ((bf16[64,8,2048]{2,1,0:T(8,128)(2,1)}), bf16[64,8,2048]{2,1,0:T(8,128)(2,1)S(1)}, u32[]{:S(2)}, u32[]{:S(2)}) async-start(bf16[64,8,2048]{2,1,0:T(8,128)(2,1)} %shard_map.147), calls=%async_computation.1 | async-start | bytes 4194304 | tf_op jit(solution)/shard_map/all_to_all | solution.py:592
  292.3 23.6 %collective-permute-start.14 = (bf16[4,80,704]{2,1,0:T(8,128)(2,1)}, bf16[4,80,704]{2,1,0:T(8,128)(2,1)S(1)}, u32[]{:S(2)}, u32[]{:S(2)}) collective-permute-start(bf16[4,80,704]{2,1,0:T(8,128)(2,1)} %get-tuple-element.20), channel_id=1, source_target_pairs={{0,1},{1,0},{2,3},{3,2},{4,5},{5,4},{6,7},{7,6},{8,9},{9,8},{10,11... | collective-permute-start | bytes 1351688 | tf_op jit(solution)/shard_map/ppermute | solution.py:578
  325.7 30.7 %all-to-all-start.3 = ((bf16[64,8,1280]{2,1,0:T(8,128)(2,1)}), bf16[64,8,1280]{2,1,0:T(8,128)(2,1)S(1)}, u32[]{:S(2)}, u32[]{:S(2)}) async-start(bf16[64,8,1280]{2,1,0:T(8,128)(2,1)} %shard_map.150), calls=%async_computation.3 | async-start | bytes 2621440 | tf_op jit(solution)/shard_map/all_to_all | solution.py:592
  (8 other events, 56.6 us)
where the time goes:
time: 367 us; the launch traced here: 362 us
  waiting for transfers between devices  189 us (51%)
  Pallas kernels  95.6 us (26%)
  starting transfers between devices  70.3 us (19%)
  local copies, waits for them, and re-layouts  5.4 us (1%)
    ppermute x3, waiting for transfers between devices, swap(): return lax.ppermute(a, 'wide', [(w, w ^ 1) for w in range(16)])  107 us
    all_to_all x2, waiting for transfers between devices, exchange(): lax.all_to_all(a, ('req', 'wide'), split_axis=0, concat_axis=0, tiled=True)  44.5 us
    all_to_all x2, starting transfers between devices, exchange(): lax.all_to_all(a, ('req', 'wide'), split_axis=0, concat_axis=0, tiled=True)  27.8 us
    pallas_call x1, Pallas kernels, attend(): pl.pallas_call(lambda *refs: attention_kernel(n_pieces, *refs), out_shape...  26.1 us
    ppermute x12, waiting for transfers between devices, hop(): return lax.ppermute(a, 'wide', shift(axis, k))  22.8 us
    all_to_all x2, starting transfers between devices, give_back(): lax.all_to_all(a, ('req', 'wide'), split_axis=0, concat_axis=0, axis_inde...  22.6 us
    pallas_call x2, Pallas kernels, run_up(): pl.pallas_call(kernel, out_shape=(jax.ShapeDtypeStruct(shape, bf16),) * 2...  21.7 us
    ppermute x12, starting transfers between devices, hop(): return lax.ppermute(a, 'wide', shift(axis, k))  17.3 us
  transfers between devices with their start and end apart: 19, of which 11 were waited for; matrix products, arithmetic and copies ran while one was open for 1% of the time, Pallas kernels for 14%

commit v1 on v0

--- a/solution.py
+++ b/solution.py
@@ -63,6 +63,10 @@
     return jnp.where(place_of(tokens, starts, bases) == slots, 1.0, 0.0).astype(bf16)
 
 
+def grant(mib):
+    return pltpu.CompilerParams(vmem_limit_bytes=mib << 20)
+
+
 def mm(a, b):
     return jnp.dot(a, b, preferred_element_type=f32)
 
@@ -109,6 +113,7 @@
             ],
         ),
         name="query_prep",
+        compiler_params=grant(24),
     )(scalars, queries, queries, w_ukv)
 
 
@@ -219,6 +224,7 @@
             ],
         ),
         name="attention",
+        compiler_params=grant(24),
     )(scalars, qa, qr, local_lat, local_rope, *pieces)
 
 
@@ -267,6 +273,7 @@
             scratch_shapes=[pltpu.VMEM((TOK, D), f32)],
         ),
         name="project",
+        compiler_params=grant(24),
     )(scalars, o_lat, w_ukv, w_out, residual, gain)
 
 
@@ -370,6 +377,7 @@
         ],
         out_specs=pl.BlockSpec((2 * EG, 8, width), lambda i: (i, 0, 0)),
         scratch_shapes=[pltpu.VMEM((EXPERTS, TOK), f32)],
+        compiler_params=grant(32),
     )(ids_t, normed)
 
 
@@ -379,10 +387,15 @@
     return gate / (1.0 + jnp.exp(-gate)) * up
 
 
+def side_of(pair, side):
+    return (side + pair // 2) % 2
+
+
 def up_kernel(side_ref, x_ref, wg_ref, own_ref, other_ref):
     n = x_ref.shape[0] // 2
     act = activate(x_ref[...].reshape(-1, D), wg_ref).reshape(n, 2, 8, HIDDEN)
-    even = side_ref[0] == 0
+    pair = lax.broadcasted_iota(jnp.int32, (n, 8, HIDDEN), 0)
+    even = side_of(pair, side_ref[0]) == 0
     own_ref[...] = jnp.where(even, act[:, 0], act[:, 1]).astype(bf16)
     other_ref[...] = jnp.where(even, act[:, 1], act[:, 0]).astype(bf16)
 
@@ -396,8 +409,14 @@
 def pick_main(n, side, half):
     r = lax.broadcasted_iota(jnp.int32, (4 * n, 16 * n), 0)
     c = lax.broadcasted_iota(jnp.int32, (4 * n, 16 * n), 1)
-    at = (2 * (r // 4) + side) * 8 + 2 * (r % 4) + half
+    at = (2 * (r // 4) + side_of(r // 4, side)) * 8 + 2 * (r % 4) + half
     return jnp.where(c == at, 1.0, 0.0).astype(bf16)
+
+
+def pick_last(n, side, q):
+    r = lax.broadcasted_iota(jnp.int32, (n, 16 * n), 0)
+    c = lax.broadcasted_iota(jnp.int32, (n, 16 * n), 1)
+    return jnp.where(c == (2 * r + side_of(r, side)) * 8 + q, 1.0, 0.0).astype(bf16)
 
 
 def up_packed_kernel(side_ref, x_ref, wg_ref, own_ref, other_ref):
@@ -412,7 +431,7 @@
     main = jnp.concatenate(halves, axis=1)
     parts = []
     for q in range(8):
-        chosen = [pick(n, 16 * n, 16, 8 * own + q), pick(n, 16 * n, 16, 8 * other + q)]
+        chosen = [pick_last(n, own, q), pick_last(n, other, q)]
         parts.append(mm(jnp.concatenate(chosen, axis=0), tail))
     last = jnp.concatenate(parts, axis=1)
     act = activate(jnp.concatenate([main, last], axis=0).astype(bf16), wg_ref).astype(bf16)
@@ -447,6 +466,7 @@
             ],
             out_specs=[pl.BlockSpec(block, lambda i, s: (i, 0, 0))] * 2,
         ),
+        compiler_params=grant(32),
     )(side, rows, w_gate_up)
 
 
@@ -481,6 +501,7 @@
         grid=(steps,),
         in_specs=[act, act, weight, weight],
         out_specs=pl.BlockSpec((EXPERTS // steps, 8, width), lambda i: (i, 0, 0)),
+        compiler_params=grant(32),
     )(own, came, w_own, w_came)
 
 
@@ -523,6 +544,7 @@
         out_specs=pl.BlockSpec((TOK, D), lambda i: (0, 0)),
         scratch_shapes=[pltpu.VMEM((EXPERTS, TOK), f32), pltpu.VMEM((EXPERTS, TOK), f32)],
         name="combine_a",
+        compiler_params=grant(32),
     )(ids_t, gates_t, hidden, back)
 
 
@@ -546,6 +568,7 @@
         out_specs=pl.BlockSpec(memory_space=pltpu.VMEM),
         scratch_shapes=[pltpu.VMEM((TOK, D), f32)],
         name="combine_b",
+        compiler_params=grant(24),
     )(ids_t, gates_t, base, back)
 
 
@@ -562,16 +585,12 @@
     return lax.ppermute(a, "wide", shift(axis, k))
 
 
-def gather_row(own, first):
-    ahead, behind = hop(own, first, 1), hop(own, first, -1)
-    far = hop(own, first, 2)
-    return jnp.concatenate([own, ahead, behind, far], axis=0)
-
-
-def gather_rest(row, second):
+def gather_blocks(own, first, second):
+    row = jnp.concatenate([own, hop(own, first, 1), hop(own, first, -1), hop(own, first, 2)], axis=0)
     ahead, behind = hop(row, second, 1), hop(row, second, -1)
-    far = hop(row, second, 2)
-    return [row, ahead, behind, far]
+    half = row.shape[0] // 2
+    far0, far1 = hop(ahead[:half], second, 1), hop(behind[half:], second, -1)
+    return [row, ahead, behind, far0, far1]
 
 
 def swap(a):
@@ -588,7 +607,7 @@
 
 
 def give_back(a):
-    sides = [list(range(side, 2 * EXPERTS, 2)) for side in range(2)]
+    sides = [[n for n in range(2 * EXPERTS) if (n + n // 4) % 2 == side] for side in range(2)]
     return lax.all_to_all(
         a, ("req", "wide"), split_axis=0, concat_axis=0, axis_index_groups=sides, tiled=True
     )
@@ -612,12 +631,11 @@
     expert_down,
 ):
     scalars = jnp.concatenate([suffix_lengths[0], prefix_ids[0]])
-    row0 = gather_row(pack_prefix(prefix_latent[0, 0], prefix_rope[0, 0]), "x")
-    row1 = gather_row(pack_prefix(prefix_latent[0, 1], prefix_rope[0, 1]), "y")
-    pieces0 = gather_rest(row0, "y")
-    pieces1 = gather_rest(row1, "x")
+    pieces0 = gather_blocks(pack_prefix(prefix_latent[0, 0], prefix_rope[0, 0]), "x", "y")
+    pieces1 = gather_blocks(pack_prefix(prefix_latent[0, 1], prefix_rope[0, 1]), "y", "x")
     down_came = swap(expert_down)
-    side = (lax.axis_index("wide") % 2).reshape(1)
+    place = lax.axis_index("wide")
+    side = ((place + place // 4) % 2).reshape(1)
     qa, qr = prepare_queries(scalars, queries, w_ukv)
     o_lat = attend(scalars, qa, qr, suffix_latent, suffix_rope, pieces0, pieces1)
     hidden, normed = project(scalars, o_lat, w_ukv, w_out, residual, norm_gain.reshape(1, D))

time: 367 us -> 333 us (0.907)
  Pallas kernels: 95.6 us -> 67.9 us
  starting transfers between devices: 70.3 us -> 59.3 us
  local copies, waits for them, and re-layouts: 5.4 us -> 15 us
  waiting for transfers between devices: 189 us -> 185 us
    unnamed x35 -> x51, local copies, waits for them, and re-layouts: 3 us -> 13.1 us
    all_to_all x2, starting transfers between devices: 27.8 us -> 18.6 us  [exchange(): lax.all_to_all(a, ('req', 'wide'), split_axis=0, concat_axis=0, tiled=True)]
    ppermute x12 -> x14, waiting for transfers between devices: 22.8 us -> 17.1 us  [hop(): return lax.ppermute(a, 'wide', shift(axis, k))]
    pallas_call x2, Pallas kernels: 8.43 us -> 3.22 us  [dispatch(): pl.pallas_call(kernel, out_shape=jax.ShapeDtypeStruct((2 * EXPERTS, 8, wi...]
    pallas_call x1, Pallas kernels: 9.52 us -> 4.54 us  [project(): pl.pallas_call(project_kernel, out_shape=(jax.ShapeDtypeStruct((TOK, D),...]
    pallas_call x2, Pallas kernels: 21.7 us -> 16.8 us  [run_up(): pl.pallas_call(kernel, out_shape=(jax.ShapeDtypeStruct(shape, bf16),) * 2...]
    pallas_call x2, Pallas kernels: 16.5 us -> 12.7 us  [run_down(): pl.pallas_call(kernel, out_shape=jax.ShapeDtypeStruct((EXPERTS, 8, width)...]
    ppermute x12 -> x14, starting transfers between devices: 17.3 us -> 16.2 us  [hop(): return lax.ppermute(a, 'wide', shift(axis, k))]
  transfers between devices with their start and end apart: 19 -> 21, of which waited for: 11 -> 10; matrix products, arithmetic and copies ran while one was open for 1% -> 0% of each run, Pallas kernels for 14% -> 11%
where the time goes in v1:
time: 333 us; the launch traced here: 328 us
  waiting for transfers between devices  185 us (56%)
  Pallas kernels  67.9 us (20%)
  starting transfers between devices  59.3 us (18%)
  local copies, waits for them, and re-layouts  15 us (5%)
    ppermute x3, waiting for transfers between devices, swap(): return lax.ppermute(a, 'wide', [(w, w ^ 1) for w in range(16)])  107 us
    all_to_all x2, waiting for transfers between devices, exchange(): lax.all_to_all(a, ('req', 'wide'), split_axis=0, concat_axis=0, tiled=True)  45.1 us
    pallas_call x1, Pallas kernels, attend(): pl.pallas_call(lambda *refs: attention_kernel(n_pieces, *refs), out_shape...  23.4 us
    all_to_all x2, starting transfers between devices, give_back(): lax.all_to_all(a, ('req', 'wide'), split_axis=0, concat_axis=0, axis_inde...  21.6 us
    all_to_all x2, starting transfers between devices, exchange(): lax.all_to_all(a, ('req', 'wide'), split_axis=0, concat_axis=0, tiled=True)  18.6 us
    ppermute x14, waiting for transfers between devices, hop(): return lax.ppermute(a, 'wide', shift(axis, k))  17.1 us
    pallas_call x2, Pallas kernels, run_up(): pl.pallas_call(kernel, out_shape=(jax.ShapeDtypeStruct(shape, bf16),) * 2...  16.8 us
    all_to_all x2, waiting for transfers between devices, give_back(): lax.all_to_all(a, ('req', 'wide'), split_axis=0, concat_axis=0, axis_inde...  16.2 us
  transfers between devices with their start and end apart: 21, of which 10 were waited for; matrix products, arithmetic and copies ran while one was open for 0% of the time, Pallas kernels for 11%

profile of v1, /device:TPU:37, one launch (start us, length us, event | category | flops | bytes accessed | tf_op | source)
XLA Modules:
  0.0 327.9 jit_solution(16773750346692700025)
XLA Ops:
  10.9 2.3 collective-permute-start.4
  16.5 11.7 %collective-permute-done.3.refs_6_ = bf16[576,512]{1,0:T(8,128)(2,1)S(1)} collective-permute-done((bf16[576,512]{1,0:T(8,128)(2,1)S(1)}, bf16[576,512]{1,0:T(8,128)(2,1)S(1)}, u32[]{:S(2)}, u32[]{:S(2)}) %collective-permute-start.3) | collective-permute-done | bytes 589856 | tf_op jit(solution)/shard_map/ppermute | solution.py:585
  28.4 2.7 collective-permute-start.6
  32.9 2.7 query_prep.1
  39.2 23.4 %attention.1.o_ref = bf16[16,128,512]{2,1,0:T(8,128)(2,1)S(1)} custom-call(s32[8]{0:T(128)S(1)} %pad_add_fusion.sc_ref.refs_0_, bf16[16,128,512]{2,1,0:T(8,128)(2,1)S(1)} %get-tuple-element.13.refs_1_, bf16[16,128,64]{2,1,0:T(8,128)(2,1)S(1)} %get-tuple-element.14.refs_2_, bf16[128,512]{1,0:T(8,128)(2,1)S(1)} %copy-done.12, bf16[64,128]{1,0:T(8,128)(2,1)S(1)} %copy-done.14, ...), custom_call_target="tpu_custom_call" | custom-call | tf_op jit(solution)/shard_map/attention/pallas_call | solution.py:205
  62.7 4.5 %project.1 = (bf16[128,2048]{1,0:T(8,128)(2,1)S(1)}, bf16[128,2048]{1,0:T(8,128)(2,1)S(1)}) custom-call(s32[8]{0:T(128)S(1)} %pad_add_fusion.sc_ref.refs_0_, bf16[16,128,512]{2,1,0:T(8,128)(2,1)S(1)} %attention.1.o_ref, bf16[512,4096]{1,0:T(8,128)(2,1)S(1)} %copy-done.3, bf16[2048,2048]{1,0:T(8,128)(2,1)S(1)} %bitcast.30, bf16[128,2048]{1,0:T(8,128)(2,1)S(1)} %copy-done.9, ...), custom_call_target="tpu_custom_call" | custom-call | tf_op jit(solution)/shard_map/project/pallas_call | solution.py:253
  69.4 2.0 copy-done.2
  71.4 11.8 %all-to-all-start = ((bf16[128,8,2048]{2,1,0:T(8,128)(2,1)}), bf16[128,8,2048]{2,1,0:T(8,128)(2,1)}, u32[]{:S(2)}, u32[]{:S(2)}) async-start(bf16[128,8,2048]{2,1,0:T(8,128)(2,1)} %copy-done.2), calls=%async_computation | async-start | bytes 8388608 | tf_op jit(solution)/shard_map/all_to_all | solution.py:606
  88.2 45.1 %all-to-all-done.x_ref = bf16[128,8,2048]{2,1,0:T(8,128)(2,1)} async-done(((bf16[128,8,2048]{2,1,0:T(8,128)(2,1)}), bf16[128,8,2048]{2,1,0:T(8,128)(2,1)}, u32[]{:S(2)}, u32[]{:S(2)}) %all-to-all-start) | async-done | bytes 4194336 | tf_op jit(solution)/shard_map/all_to_all | solution.py:606
  133.3 6.8 %all-to-all-start.2 = ((bf16[128,8,1280]{2,1,0:T(8,128)(2,1)}), bf16[128,8,1280]{2,1,0:T(8,128)(2,1)}, u32[]{:S(2)}, u32[]{:S(2)}) async-start(bf16[128,8,1280]{2,1,0:T(8,128)(2,1)} %copy-done.5), calls=%async_computation.2 | async-start | bytes 5242880 | tf_op jit(solution)/shard_map/all_to_all | solution.py:606
  140.2 2.6 copy-done
  142.8 9.0 %shard_map.146 = (bf16[64,8,704]{2,1,0:T(8,128)(2,1)S(1)}, bf16[64,8,704]{2,1,0:T(8,128)(2,1)S(1)}) custom-call(s32[1]{0:T(128)} %bitcast.10.side_ref, bf16[128,8,2048]{2,1,0:T(8,128)(2,1)} %all-to-all-done.x_ref, bf16[1,2048,1408]{2,1,0:T(8,128)(2,1)S(1)} %copy-done), custom_call_target="tpu_custom_call" | custom-call | tf_op jit(solution)/shard_map/pallas_call | solution.py:455
  153.2 59.2 %collective-permute-done.15.wc_ref = bf16[1,704,2048]{2,1,0:T(8,128)(2,1)} collective-permute-done((bf16[1,704,2048]{2,1,0:T(8,128)(2,1)S(1)}, bf16[1,704,2048]{2,1,0:T(8,128)(2,1)}, u32[]{:S(2)}, u32[]{:S(2)}) %collective-permute-start.15) | collective-permute-done | bytes 2883616 | tf_op jit(solution)/shard_map/ppermute | solution.py:597
  212.4 23.8 %collective-permute-done.14.came_ref = bf16[64,8,704]{2,1,0:T(8,128)(2,1)S(1)} collective-permute-done((bf16[64,8,704]{2,1,0:T(8,128)(2,1)S(1)}, bf16[64,8,704]{2,1,0:T(8,128)(2,1)S(1)}, u32[]{:S(2)}, u32[]{:S(2)}) %collective-permute-start.14) | collective-permute-done | bytes 720928 | tf_op jit(solution)/shard_map/ppermute | solution.py:597
  236.2 5.4 %shard_map.147 = bf16[64,8,2048]{2,1,0:T(8,128)(2,1)S(1)} custom-call(bf16[64,8,704]{2,1,0:T(8,128)(2,1)S(1)} %get-tuple-element.17.own_ref, bf16[64,8,704]{2,1,0:T(8,128)(2,1)S(1)} %collective-permute-done.14.came_ref, bf16[1,704,2048]{2,1,0:T(8,128)(2,1)S(1)} %copy-done.4, bf16[1,704,2048]{2,1,0:T(8,128)(2,1)} %collective-permute-done.15.wc_ref), custom_call_target="tpu_custom_call" | custom-call | tf_op jit(solution)/shard_map/pallas_call | solution.py:498
  243.0 10.6 %all-to-all-start.1 = ((bf16[64,8,2048]{2,1,0:T(8,128)(2,1)}), bf16[64,8,2048]{2,1,0:T(8,128)(2,1)}, u32[]{:S(2)}, u32[]{:S(2)}) async-start(bf16[64,8,2048]{2,1,0:T(8,128)(2,1)} %copy-done.6), calls=%async_computation.1 | async-start | bytes 4194304 | tf_op jit(solution)/shard_map/all_to_all | solution.py:611
  253.6 2.6 copy-done.1
  256.2 7.8 %shard_map.149 = (bf16[4,80,704]{2,1,0:T(8,128)(2,1)S(1)}, bf16[4,80,704]{2,1,0:T(8,128)(2,1)S(1)}) custom-call(s32[1]{0:T(128)} %bitcast.10.side_ref, bf16[128,8,1280]{2,1,0:T(8,128)(2,1)} %all-to-all-done.2.x_ref, bf16[1,2048,1408]{2,1,0:T(8,128)(2,1)S(1)} %copy-done.1), custom_call_target="tpu_custom_call" | custom-call | tf_op jit(solution)/shard_map/pallas_call | solution.py:455
  264.1 23.5 %collective-permute-done.16.came_ref = bf16[4,80,704]{2,1,0:T(8,128)(2,1)S(1)} collective-permute-done((bf16[4,80,704]{2,1,0:T(8,128)(2,1)S(1)}, bf16[4,80,704]{2,1,0:T(8,128)(2,1)S(1)}, u32[]{:S(2)}, u32[]{:S(2)}) %collective-permute-start.16) | collective-permute-done | bytes 450592 | tf_op jit(solution)/shard_map/ppermute | solution.py:597
  287.6 7.2 %shard_map.150 = bf16[64,8,1280]{2,1,0:T(8,128)(2,1)S(1)} custom-call(bf16[4,80,704]{2,1,0:T(8,128)(2,1)S(1)} %get-tuple-element.19.own_ref, bf16[4,80,704]{2,1,0:T(8,128)(2,1)S(1)} %collective-permute-done.16.came_ref, bf16[1,704,2048]{2,1,0:T(8,128)(2,1)S(1)} %copy-done.4, bf16[1,704,2048]{2,1,0:T(8,128)(2,1)} %collective-permute-done.15.wc_ref), custom_call_target="tpu_custom_call" | custom-call | tf_op jit(solution)/shard_map/pallas_call | solution.py:498
  296.0 11.0 %all-to-all-start.3 = ((bf16[64,8,1280]{2,1,0:T(8,128)(2,1)}), bf16[64,8,1280]{2,1,0:T(8,128)(2,1)S(1)}, u32[]{:S(2)}, u32[]{:S(2)}) async-start(bf16[64,8,1280]{2,1,0:T(8,128)(2,1)} %copy-done.7), calls=%async_computation.3 | async-start | bytes 2621440 | tf_op jit(solution)/shard_map/all_to_all | solution.py:611
  307.0 2.4 combine_a.1.sum_ref
  309.3 16.2 %all-to-all-done.3.back_ref = bf16[64,8,1280]{2,1,0:T(8,128)(2,1)S(1)} async-done(((bf16[64,8,1280]{2,1,0:T(8,128)(2,1)}), bf16[64,8,1280]{2,1,0:T(8,128)(2,1)S(1)}, u32[]{:S(2)}, u32[]{:S(2)}) %all-to-all-start.3) | async-done | bytes 1310752 | tf_op jit(solution)/shard_map/all_to_all | solution.py:611
  325.6 2.3 combine_b.1
  (95 shorter events, 30.5 us)
Async XLA Ops:
  1.8 31.0 %copy-start.16 = (bf16[2048]{0:T(1024)(128)(2,1)S(1)}, bf16[2048]{0:T(1024)(128)(2,1)}, u32[]{:S(2)}) copy-start(bf16[2048]{0:T(1024)(128)(2,1)} %param.25) | copy-start | bytes 12292
  1.8 31.1 %copy-start.3 = (bf16[512,4096]{1,0:T(8,128)(2,1)S(1)}, bf16[512,4096]{1,0:T(8,128)(2,1)}, u32[]{:S(2)}) copy-start(bf16[512,4096]{1,0:T(8,128)(2,1)} %w_ref.3) | copy-start | bytes 12582916
  1.8 31.1 %copy-start.8 = (bf16[128,3072]{1,0:T(8,128)(2,1)S(1)}, bf16[128,3072]{1,0:T(8,128)(2,1)}, u32[]{:S(2)}) copy-start(bf16[128,3072]{1,0:T(8,128)(2,1)} %qr_ref.1) | copy-start | bytes 2359300
  1.8 6.9 %collective-permute-start = (bf16[144,512]{1,0:T(8,128)(2,1)S(1)}, bf16[144,512]{1,0:T(8,128)(2,1)S(1)}, u32[]{:S(2)}, u32[]{:S(2)}) collective-permute-start(bf16[144,512]{1,0:T(8,128)(2,1)S(1)} %pad_maximum_fusion), channel_id=1, source_target_pairs={{0,4},{1,5},{2,6},{3,7},{4,8},{5,9},{6,10},{7,11},{8,12},{9,13},{1... | collective-permute-start | bytes 442376 | tf_op jit(solution)/shard_map/ppermute | solution.py:585
  2.8 7.6 %collective-permute-start.1 = (bf16[144,512]{1,0:T(8,128)(2,1)S(1)}, bf16[144,512]{1,0:T(8,128)(2,1)S(1)}, u32[]{:S(2)}, u32[]{:S(2)}) collective-permute-start(bf16[144,512]{1,0:T(8,128)(2,1)S(1)} %pad_maximum_fusion), channel_id=1, source_target_pairs={{0,12},{1,13},{2,14},{3,15},{4,0},{5,1},{6,2},{7,3},{8,4},{9,5},{1... | collective-permute-start | bytes 442376 | tf_op jit(solution)/shard_map/ppermute | solution.py:585
  3.4 7.1 %collective-permute-start.2 = (bf16[144,512]{1,0:T(8,128)(2,1)S(1)}, bf16[144,512]{1,0:T(8,128)(2,1)S(1)}, u32[]{:S(2)}, u32[]{:S(2)}) collective-permute-start(bf16[144,512]{1,0:T(8,128)(2,1)S(1)} %pad_maximum_fusion), channel_id=1, source_target_pairs={{0,8},{1,9},{2,10},{3,11},{4,12},{5,13},{6,14},{7,15},{8,0},{9,1},... | collective-permute-start | bytes 442376 | tf_op jit(solution)/shard_map/ppermute | solution.py:585
  4.8 8.4 %collective-permute-start.7 = (bf16[144,512]{1,0:T(8,128)(2,1)S(1)}, bf16[144,512]{1,0:T(8,128)(2,1)S(1)}, u32[]{:S(2)}, u32[]{:S(2)}) collective-permute-start(bf16[144,512]{1,0:T(8,128)(2,1)S(1)} %pad_maximum_fusion.1), channel_id=1, source_target_pairs={{0,1},{1,2},{2,3},{3,0},{4,5},{5,6},{6,7},{7,4},{8,9},{9,10},{10,1... | collective-permute-start | bytes 442376 | tf_op jit(solution)/shard_map/ppermute | solution.py:585
  6.2 7.0 %collective-permute-start.8 = (bf16[144,512]{1,0:T(8,128)(2,1)S(1)}, bf16[144,512]{1,0:T(8,128)(2,1)S(1)}, u32[]{:S(2)}, u32[]{:S(2)}) collective-permute-start(bf16[144,512]{1,0:T(8,128)(2,1)S(1)} %pad_maximum_fusion.1), channel_id=1, source_target_pairs={{0,3},{1,0},{2,1},{3,2},{4,7},{5,4},{6,5},{7,6},{8,11},{9,8},{10,9... | collective-permute-start | bytes 442376 | tf_op jit(solution)/shard_map/ppermute | solution.py:585
  8.8 6.2 %collective-permute-start.9 = (bf16[144,512]{1,0:T(8,128)(2,1)S(1)}, bf16[144,512]{1,0:T(8,128)(2,1)S(1)}, u32[]{:S(2)}, u32[]{:S(2)}) collective-permute-start(bf16[144,512]{1,0:T(8,128)(2,1)S(1)} %pad_maximum_fusion.1), channel_id=1, source_target_pairs={{0,2},{1,3},{2,0},{3,1},{4,6},{5,7},{6,4},{7,5},{8,10},{9,11},{10,... | collective-permute-start | bytes 442376 | tf_op jit(solution)/shard_map/ppermute | solution.py:585
  10.5 17.8 %collective-permute-start.3 = (bf16[576,512]{1,0:T(8,128)(2,1)S(1)}, bf16[576,512]{1,0:T(8,128)(2,1)S(1)}, u32[]{:S(2)}, u32[]{:S(2)}) collective-permute-start(bf16[576,512]{1,0:T(8,128)(2,1)S(1)} %constant_dynamic-update-slice_fusion.refs_5_), channel_id=1, source_target_pairs={{0,1},{1,2},{2,3},{3,0},{4,5},{5,6},{6,7},{7,4},{8,9},{9,10},{10,1... | collective-permute-start | bytes 1769480 | tf_op jit(solution)/shard_map/ppermute | solution.py:585
  10.9 17.4 %collective-permute-start.4 = (bf16[576,512]{1,0:T(8,128)(2,1)S(1)}, bf16[576,512]{1,0:T(8,128)(2,1)S(1)}, u32[]{:S(2)}, u32[]{:S(2)}) collective-permute-start(bf16[576,512]{1,0:T(8,128)(2,1)S(1)} %constant_dynamic-update-slice_fusion.refs_5_), channel_id=1, source_target_pairs={{0,3},{1,0},{2,1},{3,2},{4,7},{5,4},{6,5},{7,6},{8,11},{9,8},{10,9... | collective-permute-start | bytes 1769480 | tf_op jit(solution)/shard_map/ppermute | solution.py:585
  15.0 16.1 %collective-permute-start.10 = (bf16[576,512]{1,0:T(8,128)(2,1)S(1)}, bf16[576,512]{1,0:T(8,128)(2,1)S(1)}, u32[]{:S(2)}, u32[]{:S(2)}) collective-permute-start(bf16[576,512]{1,0:T(8,128)(2,1)S(1)} %constant_dynamic-update-slice_fusion.5.refs_10_), channel_id=1, source_target_pairs={{0,4},{1,5},{2,6},{3,7},{4,8},{5,9},{6,10},{7,11},{8,12},{9,13},{1... | collective-permute-start | bytes 1769480 | tf_op jit(solution)/shard_map/ppermute | solution.py:585
  15.6 16.5 %collective-permute-start.11 = (bf16[576,512]{1,0:T(8,128)(2,1)S(1)}, bf16[576,512]{1,0:T(8,128)(2,1)S(1)}, u32[]{:S(2)}, u32[]{:S(2)}) collective-permute-start(bf16[576,512]{1,0:T(8,128)(2,1)S(1)} %constant_dynamic-update-slice_fusion.5.refs_10_), channel_id=1, source_target_pairs={{0,12},{1,13},{2,14},{3,15},{4,0},{5,1},{6,2},{7,3},{8,4},{9,5},{1... | collective-permute-start | bytes 1769480 | tf_op jit(solution)/shard_map/ppermute | solution.py:585
  28.3 8.3 %collective-permute-start.5 = (bf16[288,512]{1,0:T(8,128)(2,1)S(1)}, bf16[288,512]{1,0:T(8,128)(2,1)S(1)}, u32[]{:S(2)}, u32[]{:S(2)}) collective-permute-start(bf16[288,512]{1,0:T(8,128)(2,1)S(1)} %slice.32), channel_id=1, source_target_pairs={{0,1},{1,2},{2,3},{3,0},{4,5},{5,6},{6,7},{7,4},{8,9},{9,10},{10,1... | collective-permute-start | bytes 884744 | tf_op jit(solution)/shard_map/ppermute | solution.py:585
  28.4 8.2 %collective-permute-start.6 = (bf16[288,512]{1,0:T(8,128)(2,1)S(1)}, bf16[288,512]{1,0:T(8,128)(2,1)S(1)}, u32[]{:S(2)}, u32[]{:S(2)}) collective-permute-start(bf16[288,512]{1,0:T(8,128)(2,1)S(1)} %slice.33), channel_id=1, source_target_pairs={{0,3},{1,0},{2,1},{3,2},{4,7},{5,4},{6,5},{7,6},{8,11},{9,8},{10,9... | collective-permute-start | bytes 884744 | tf_op jit(solution)/shard_map/ppermute | solution.py:585
  31.2 6.5 %collective-permute-start.12 = (bf16[288,512]{1,0:T(8,128)(2,1)S(1)}, bf16[288,512]{1,0:T(8,128)(2,1)S(1)}, u32[]{:S(2)}, u32[]{:S(2)}) collective-permute-start(bf16[288,512]{1,0:T(8,128)(2,1)S(1)} %slice.34), channel_id=1, source_target_pairs={{0,4},{1,5},{2,6},{3,7},{4,8},{5,9},{6,10},{7,11},{8,12},{9,13},{1... | collective-permute-start | bytes 884744 | tf_op jit(solution)/shard_map/ppermute | solution.py:585
  32.2 7.1 %collective-permute-start.13 = (bf16[288,512]{1,0:T(8,128)(2,1)S(1)}, bf16[288,512]{1,0:T(8,128)(2,1)S(1)}, u32[]{:S(2)}, u32[]{:S(2)}) collective-permute-start(bf16[288,512]{1,0:T(8,128)(2,1)S(1)} %slice.35), channel_id=1, source_target_pairs={{0,12},{1,13},{2,14},{3,15},{4,0},{5,1},{6,2},{7,3},{8,4},{9,5},{1... | collective-permute-start | bytes 884744 | tf_op jit(solution)/shard_map/ppermute | solution.py:585
  71.4 61.9 %all-to-all-start = ((bf16[128,8,2048]{2,1,0:T(8,128)(2,1)}), bf16[128,8,2048]{2,1,0:T(8,128)(2,1)}, u32[]{:S(2)}, u32[]{:S(2)}) async-start(bf16[128,8,2048]{2,1,0:T(8,128)(2,1)} %copy-done.2), calls=%async_computation | async-start | bytes 8388608 | tf_op jit(solution)/shard_map/all_to_all | solution.py:606
  83.3 129.2 %collective-permute-start.15 = (bf16[1,704,2048]{2,1,0:T(8,128)(2,1)S(1)}, bf16[1,704,2048]{2,1,0:T(8,128)(2,1)}, u32[]{:S(2)}, u32[]{:S(2)}) collective-permute-start(bf16[1,704,2048]{2,1,0:T(8,128)(2,1)S(1)} %copy-done.4), channel_id=1, source_target_pairs={{0,1},{1,0},{2,3},{3,2},{4,5},{5,4},{6,7},{7,6},{8,9},{9,8},{10,11... | collective-permute-start | bytes 8650760 | tf_op jit(solution)/shard_map/ppermute | solution.py:597
  133.3 109.6 %all-to-all-start.2 = ((bf16[128,8,1280]{2,1,0:T(8,128)(2,1)}), bf16[128,8,1280]{2,1,0:T(8,128)(2,1)}, u32[]{:S(2)}, u32[]{:S(2)}) async-start(bf16[128,8,1280]{2,1,0:T(8,128)(2,1)} %copy-done.5), calls=%async_computation.2 | async-start | bytes 5242880 | tf_op jit(solution)/shard_map/all_to_all | solution.py:606
  151.9 84.3 %collective-permute-start.14 = (bf16[64,8,704]{2,1,0:T(8,128)(2,1)S(1)}, bf16[64,8,704]{2,1,0:T(8,128)(2,1)S(1)}, u32[]{:S(2)}, u32[]{:S(2)}) collective-permute-start(bf16[64,8,704]{2,1,0:T(8,128)(2,1)S(1)} %get-tuple-element.18), channel_id=1, source_target_pairs={{0,1},{1,0},{2,3},{3,2},{4,5},{5,4},{6,7},{7,6},{8,9},{9,8},{10,11... | collective-permute-start | bytes 2162696 | tf_op jit(solution)/shard_map/ppermute | solution.py:597
  243.0 53.0 %all-to-all-start.1 = ((bf16[64,8,2048]{2,1,0:T(8,128)(2,1)}), bf16[64,8,2048]{2,1,0:T(8,128)(2,1)}, u32[]{:S(2)}, u32[]{:S(2)}) async-start(bf16[64,8,2048]{2,1,0:T(8,128)(2,1)} %copy-done.6), calls=%async_computation.1 | async-start | bytes 4194304 | tf_op jit(solution)/shard_map/all_to_all | solution.py:611
  264.0 23.6 %collective-permute-start.16 = (bf16[4,80,704]{2,1,0:T(8,128)(2,1)S(1)}, bf16[4,80,704]{2,1,0:T(8,128)(2,1)S(1)}, u32[]{:S(2)}, u32[]{:S(2)}) collective-permute-start(bf16[4,80,704]{2,1,0:T(8,128)(2,1)S(1)} %get-tuple-element.20), channel_id=1, source_target_pairs={{0,1},{1,0},{2,3},{3,2},{4,5},{5,4},{6,7},{7,6},{8,9},{9,8},{10,11... | collective-permute-start | bytes 1351688 | tf_op jit(solution)/shard_map/ppermute | solution.py:597
  296.0 29.6 %all-to-all-start.3 = ((bf16[64,8,1280]{2,1,0:T(8,128)(2,1)}), bf16[64,8,1280]{2,1,0:T(8,128)(2,1)S(1)}, u32[]{:S(2)}, u32[]{:S(2)}) async-start(bf16[64,8,1280]{2,1,0:T(8,128)(2,1)} %copy-done.7), calls=%async_computation.3 | async-start | bytes 2621440 | tf_op jit(solution)/shard_map/all_to_all | solution.py:611
  (18 other events, 202.5 us)
